TPU v7x, 32 devices: a whole 2x2x4 slice. The times are simulated.
32 devices in a mesh: span: 4 (over z), flow: 8 (over y, x, core).
Axes of the slice: x: 2, y: 2, z: 4, core: 2. Of those that a mesh axis runs over, the one named last changes fastest.
Arguments:
- rhs_fluid: float32 [6, 8, 64, 128], P(None, 'span', 'flow'), may hold values from -6 to 6
- rhs_solid: float32 [32, 128], P('span'), may hold values from -6 to 6
- blocks: float32 [6, 6, 8, 64, 128], P(None, None, 'span', 'flow')
- weights: float32 [6, 8, 64, 128], P(None, 'span', 'flow'), may hold values from 0.5 to 1.1
- kdiag: float32 [32, 128], P('span'), may hold values from 1 to 4
- wall_fluid: int32 [4, 8], P('span', 'flow'), may hold values from 0 to 15
- wall_solid: int32 [4, 8], P('span', 'flow'), may hold values from 0 to 7, each once within a row
- wall_coef: float32 [4, 8, 128], P('span', 'flow'), may hold values from 0.3 to 1.5
Outputs:
- x_fluid: float32 [6, 8, 64, 128], P(None, 'span', 'flow')
- x_solid: float32 [32, 128], P('span')
Inputs may be any that keep to these rules, and one draw needn't show every extreme that they name: `wall_fluid`: a local row a * 8 + b of the fluid tile of span index i and flow index q; rows may repeat. `wall_solid`: each row is a permutation of the 8 metal rows of band i.
All inputs are finite; a program needn't handle non-finite values.
Results may differ from a plain program's by a relative error of at most 0.0003.
Values sent between devices are 32-bit elements; how exact they have to be, the bound alone decides.
No kernel may reach another device: no remote copies, remote signals or barrier semaphores. Data moves between devices by JAX's collectives and lax.ppermute only.
A program may use at most 64 MiB of HBM per device.

v0:
```python
import jax
import jax.numpy as jnp
from jax import lax
from jax.sharding import PartitionSpec as P

KRYLOV = 6


def extended(shard, sides, width):
    for axis, dim in sides:
        count, length = (lax.axis_size(axis), shard.shape[dim])
        up = [(i, (i + 1) % count) for i in range(count - 1)]
        down = [(j, i) for i, j in up]
        last = lax.slice_in_dim(shard, length - width, length, axis=dim)
        first = lax.slice_in_dim(shard, 0, width, axis=dim)
        before = lax.ppermute(last, axis, up)
        after = lax.ppermute(first, axis, down)
        shard = jnp.concatenate([before, shard, after], axis=dim)
    return shard


def least_squares(hess, beta, steps):
    cos_list, sin_list, upper = ([], [], [])
    rhs_g = [beta] + [jnp.float32(0.0) for _ in range(steps)]
    for j in range(steps):
        column = [hess[i][j] for i in range(j + 2)]
        for i in range(j):
            top = cos_list[i] * column[i] + sin_list[i] * column[i + 1]
            column[i + 1] = -sin_list[i] * column[i] + cos_list[i] * column[i + 1]
            column[i] = top
        radius = jnp.sqrt(column[j] * column[j] + column[j + 1] * column[j + 1])
        cos_now = column[j] / radius
        sin_now = column[j + 1] / radius
        column[j] = radius
        rhs_g[j + 1] = -sin_now * rhs_g[j]
        rhs_g[j] = cos_now * rhs_g[j]
        cos_list.append(cos_now)
        sin_list.append(sin_now)
        upper.append(column[: j + 1])
    coeffs = [None] * steps
    for j in range(steps - 1, -1, -1):
        total = rhs_g[j]
        for k in range(j + 1, steps):
            total = total - upper[k][j] * coeffs[k]
        coeffs[j] = total / upper[j][j]
    return coeffs


def shards(rhs_fluid, rhs_solid, blocks, weights, kdiag, wall_fluid, wall_solid, wall_coef):
    rows_a = rhs_fluid.shape[1]
    rows_b = rhs_fluid.shape[2]
    width = rhs_fluid.shape[3]
    cells = rows_a * rows_b
    band_rows = rhs_solid.shape[0]
    patch_rows = wall_fluid[0]
    patch_metal = wall_solid[0]
    coef = wall_coef[0]
    fluid_pick = (jnp.arange(cells, dtype=jnp.int32)[:, None] == patch_rows[None, :]).astype(
        jnp.float32
    )
    metal_pick = (jnp.arange(band_rows, dtype=jnp.int32)[:, None] == patch_metal[None, :]).astype(
        jnp.float32
    )
    first_flow = (lax.axis_index("flow") == 0).astype(jnp.float32)
    highest = lax.Precision.HIGHEST

    def local_inner(left, right):
        return jnp.sum(left[0] * right[0]) + first_flow * jnp.sum(left[1] * right[1])

    beta = jnp.sqrt(
        lax.psum(local_inner((rhs_fluid, rhs_solid), (rhs_fluid, rhs_solid)), ("span", "flow"))
    )
    basis = [(rhs_fluid / beta, rhs_solid / beta)]
    hess = [[jnp.float32(0.0) for _ in range(KRYLOV)] for _ in range(KRYLOV + 1)]
    for j in range(KRYLOV):
        field = basis[j][0]
        metal_u = basis[j][1]
        padded = extended(field, (("span", 1), ("flow", 2)), 1)
        local = jnp.einsum("fgabc,gabc->fabc", blocks, field, precision=highest)
        beside = weights[0][None] * padded[:, :-2, 1:-1] + weights[1][None] * padded[:, 2:, 1:-1]
        beside = (
            beside
            + weights[2][None] * padded[:, 1:-1, :-2]
            + weights[3][None] * padded[:, 1:-1, 2:]
        )
        beside = (
            beside
            + weights[4][None] * jnp.roll(field, 1, axis=3)
            + weights[5][None] * jnp.roll(field, -1, axis=3)
        )
        metal_at = jnp.dot(metal_pick.T, metal_u, precision=highest)
        inflow = jnp.dot(fluid_pick, coef * metal_at, precision=highest).reshape(
            rows_a, rows_b, width
        )
        image_f = (local - beside).at[5].add(-inflow)
        wall_vals = coef * jnp.dot(fluid_pick.T, field[5].reshape(cells, width), precision=highest)
        sink = lax.psum(jnp.dot(metal_pick, wall_vals, precision=highest), "flow")
        upad = extended(metal_u, (("span", 0),), 1)
        beside_all = (
            upad[:-2] + upad[2:] + jnp.roll(metal_u, 1, axis=1) + jnp.roll(metal_u, -1, axis=1)
        )
        image_s = (4.0 + kdiag) * metal_u - beside_all - sink
        image_f, image_s = (image_f, image_s)
        terms = jnp.stack([local_inner(basis[i], (image_f, image_s)) for i in range(j + 1)])
        values = lax.psum(terms, ("span", "flow"))
        for i in range(j + 1):
            image_f = image_f - values[i] * basis[i][0]
            image_s = image_s - values[i] * basis[i][1]
        rest = jnp.sqrt(
            lax.psum(local_inner((image_f, image_s), (image_f, image_s)), ("span", "flow"))
        )
        for i in range(j + 1):
            hess[i][j] = values[i]
        hess[j + 1][j] = rest
        basis.append((image_f / rest, image_s / rest))
    coeffs = least_squares(hess, beta, KRYLOV)
    x_fluid = jnp.zeros_like(rhs_fluid)
    x_solid = jnp.zeros_like(rhs_solid)
    for j in range(KRYLOV):
        x_fluid = x_fluid + coeffs[j] * basis[j][0]
        x_solid = x_solid + coeffs[j] * basis[j][1]
    return (x_fluid, x_solid)


def solution(mesh):
    in_specs = (
        P(None, "span", "flow", None),
        P("span", None),
        P(None, None, "span", "flow", None),
        P(None, "span", "flow", None),
        P("span", None),
        P("span", "flow"),
        P("span", "flow"),
        P("span", "flow", None),
    )
    out_specs = (P(None, "span", "flow", None), P("span", None))
    return jax.shard_map(shards, mesh=mesh, in_specs=in_specs, out_specs=out_specs, check_vma=False)
```

profile of v0, /device:TPU:0, one launch (start us, length us, event | category | flops | bytes accessed | tf_op | source)
XLA Modules:
  0.0 832.7 jit_solution(11457681903520337118)
XLA Ops:
  4.6 42.0 %psum.133 = f32[]{:T(128)} all-reduce(f32[]{:T(128)S(6)} %add.455), channel_id=1, replica_groups=mesh['span'=4,'flow'=8] {'span','flow'}, use_global_device_ids=true, to_apply=%region_2.0 | all-reduce | flops 1 | bytes 8 | tf_op jit(solution)/shard_map/psum | solution.py:71
  47.4 3.4 collective-permute-start
  52.1 4.5 collective-permute-start.4
  56.7 1.4 collective-permute-start.5
  61.4 12.0 %psum.134 = f32[8,128]{1,0:T(8,128)S(1)} all-reduce(f32[8,128]{1,0:T(8,128)S(1)} %broadcast_multiply_fusion.5), channel_id=1, replica_groups=mesh['span'=4,'flow'=8] {'flow'}, use_global_device_ids=true, to_apply=%region_4.5 | all-reduce | flops 1024 | bytes 8192 | tf_op jit(solution)/shard_map/psum | solution.py:97
  73.5 1.5 collective-permute-start.2
  80.2 44.8 %psum.135 = f32[]{:T(128)} all-reduce(f32[]{:T(128)S(6)} %add.466), channel_id=1, replica_groups=mesh['span'=4,'flow'=8] {'span','flow'}, use_global_device_ids=true, to_apply=%region_6.7 | all-reduce | flops 1 | bytes 8 | tf_op jit(solution)/shard_map/psum | solution.py:105
  128.8 39.3 %psum.136 = f32[]{:T(128)} all-reduce(f32[]{:T(128)S(6)} %add.467), channel_id=1, replica_groups=mesh['span'=4,'flow'=8] {'span','flow'}, use_global_device_ids=true, to_apply=%region_9.10 | all-reduce | flops 1 | bytes 8 | tf_op jit(solution)/shard_map/psum | solution.py:110
  170.5 3.5 collective-permute-start.10
  175.6 4.6 collective-permute-start.6
  183.7 12.1 %psum.137 = f32[8,128]{1,0:T(8,128)S(1)} all-reduce(f32[8,128]{1,0:T(8,128)S(1)} %broadcast_multiply_fusion.4), channel_id=1, replica_groups=mesh['span'=4,'flow'=8] {'flow'}, use_global_device_ids=true, to_apply=%region_11.12 | all-reduce | flops 1024 | bytes 8192 | tf_op jit(solution)/shard_map/psum | solution.py:97
  195.8 2.3 collective-permute-start.8
  203.7 44.3 %psum.138 = f32[2]{0:T(128)S(1)} all-reduce(f32[2]{0:T(128)S(1)} %pad_maximum_fusion.78), channel_id=1, replica_groups=mesh['span'=4,'flow'=8] {'span','flow'}, use_global_device_ids=true, to_apply=%region_15.16 | all-reduce | flops 2 | bytes 16 | tf_op jit(solution)/shard_map/psum | solution.py:105
  248.5 1.9 multiply_reduce_fusion.28
  250.4 1.9 multiply_reduce_fusion.56
  253.6 39.5 %psum.139 = f32[]{:T(128)} all-reduce(f32[]{:T(128)S(6)} %add.482), channel_id=1, replica_groups=mesh['span'=4,'flow'=8] {'span','flow'}, use_global_device_ids=true, to_apply=%region_18.19 | all-reduce | flops 1 | bytes 8 | tf_op jit(solution)/shard_map/psum | solution.py:110
  294.5 3.6 collective-permute-start.12
  302.1 4.5 collective-permute-start.16
  307.9 12.1 %psum.140 = f32[8,128]{1,0:T(8,128)S(1)} all-reduce(f32[8,128]{1,0:T(8,128)S(1)} %broadcast_multiply_fusion.3), channel_id=1, replica_groups=mesh['span'=4,'flow'=8] {'flow'}, use_global_device_ids=true, to_apply=%region_20.21 | all-reduce | flops 1024 | bytes 8192 | tf_op jit(solution)/shard_map/psum | solution.py:97
  320.0 1.7 collective-permute-start.14
  328.7 44.2 %psum.141 = f32[3]{0:T(128)S(1)} all-reduce(f32[3]{0:T(128)S(1)} %pad_maximum_fusion.79), channel_id=1, replica_groups=mesh['span'=4,'flow'=8] {'span','flow'}, use_global_device_ids=true, to_apply=%region_26.27 | all-reduce | flops 3 | bytes 24 | tf_op jit(solution)/shard_map/psum | solution.py:105
  373.5 2.6 multiply_reduce_fusion.24
  376.0 2.5 multiply_reduce_fusion.52
  379.8 40.0 %psum.142 = f32[]{:T(128)} all-reduce(f32[]{:T(128)S(6)} %add.499), channel_id=1, replica_groups=mesh['span'=4,'flow'=8] {'span','flow'}, use_global_device_ids=true, to_apply=%region_29.30 | all-reduce | flops 1 | bytes 8 | tf_op jit(solution)/shard_map/psum | solution.py:110
  423.3 3.6 collective-permute-start.22
  428.6 4.6 collective-permute-start.18
  436.0 12.1 %psum.143 = f32[8,128]{1,0:T(8,128)S(1)} all-reduce(f32[8,128]{1,0:T(8,128)S(1)} %broadcast_multiply_fusion.2), channel_id=1, replica_groups=mesh['span'=4,'flow'=8] {'flow'}, use_global_device_ids=true, to_apply=%region_31.32 | all-reduce | flops 1024 | bytes 8192 | tf_op jit(solution)/shard_map/psum | solution.py:97
  448.1 1.5 collective-permute-start.20
  457.7 44.2 %psum.144 = f32[4]{0:T(128)S(1)} all-reduce(f32[4]{0:T(128)S(1)} %pad_maximum_fusion.80), channel_id=1, replica_groups=mesh['span'=4,'flow'=8] {'span','flow'}, use_global_device_ids=true, to_apply=%region_39.40 | all-reduce | flops 4 | bytes 32 | tf_op jit(solution)/shard_map/psum | solution.py:105
  502.6 3.2 multiply_reduce_fusion.19
  505.8 3.1 multiply_reduce_fusion.47
  510.2 40.2 %psum.145 = f32[]{:T(128)} all-reduce(f32[]{:T(128)S(6)} %add.518), channel_id=1, replica_groups=mesh['span'=4,'flow'=8] {'span','flow'}, use_global_device_ids=true, to_apply=%region_42.43 | all-reduce | flops 1 | bytes 8 | tf_op jit(solution)/shard_map/psum | solution.py:110
  554.5 3.6 collective-permute-start.28
  559.7 4.6 collective-permute-start.24
  567.8 12.1 %psum.146 = f32[8,128]{1,0:T(8,128)S(1)} all-reduce(f32[8,128]{1,0:T(8,128)S(1)} %broadcast_multiply_fusion.1), channel_id=1, replica_groups=mesh['span'=4,'flow'=8] {'flow'}, use_global_device_ids=true, to_apply=%region_44.45 | all-reduce | flops 1024 | bytes 8192 | tf_op jit(solution)/shard_map/psum | solution.py:97
  579.9 1.5 collective-permute-start.26
  590.8 44.4 %psum.147 = f32[5]{0:T(128)S(1)} all-reduce(f32[5]{0:T(128)S(1)} %stack.96), channel_id=1, replica_groups=mesh['span'=4,'flow'=8] {'span','flow'}, use_global_device_ids=true, to_apply=%region_54.55 | all-reduce | flops 5 | bytes 40 | tf_op jit(solution)/shard_map/psum | solution.py:105
  635.8 3.8 multiply_reduce_fusion.13
  639.6 3.7 multiply_reduce_fusion.41
  644.5 40.2 %psum.148 = f32[]{:T(128)} all-reduce(f32[]{:T(128)S(6)} %add.539), channel_id=1, replica_groups=mesh['span'=4,'flow'=8] {'span','flow'}, use_global_device_ids=true, to_apply=%region_57.58 | all-reduce | flops 1 | bytes 8 | tf_op jit(solution)/shard_map/psum | solution.py:110
  688.9 3.6 collective-permute-start.34
  694.2 4.6 collective-permute-start.30
  703.3 12.1 %psum.149 = f32[8,128]{1,0:T(8,128)S(1)} all-reduce(f32[8,128]{1,0:T(8,128)S(1)} %broadcast_multiply_fusion), channel_id=1, replica_groups=mesh['span'=4,'flow'=8] {'flow'}, use_global_device_ids=true, to_apply=%region_59.60 | all-reduce | flops 1024 | bytes 8192 | tf_op jit(solution)/shard_map/psum | solution.py:97
  715.4 1.5 collective-permute-start.32
  727.6 44.2 %psum.150 = f32[6]{0:T(128)S(1)} all-reduce(f32[6]{0:T(128)S(1)} %stack.103), channel_id=1, replica_groups=mesh['span'=4,'flow'=8] {'span','flow'}, use_global_device_ids=true, to_apply=%region_71.72 | all-reduce | flops 6 | bytes 48 | tf_op jit(solution)/shard_map/psum | solution.py:105
  775.6 4.4 multiply_reduce_fusion.6
  784.4 4.3 multiply_reduce_fusion.34
  790.1 40.2 %psum.151 = f32[]{:T(128)} all-reduce(f32[]{:T(128)S(6)} %add.562), channel_id=1, replica_groups=mesh['span'=4,'flow'=8] {'span','flow'}, use_global_device_ids=true, to_apply=%region_74.75 | all-reduce | flops 1 | bytes 8 | tf_op jit(solution)/shard_map/psum | solution.py:110
  (190 shorter events, 49.7 us)
Async XLA Ops:
  0.6 0.7 copy-start.2
  0.6 46.7 %copy-start = (f32[6,2,8,128]{3,2,1,0:T(8,128)S(1)}, f32[6,2,8,128]{3,2,1,0:T(8,128)}, u32[]{:S(2)}) copy-start(f32[6,2,8,128]{3,2,1,0:T(8,128)} %param.20) | copy-start | bytes 147460
  47.4 26.1 %collective-permute-start = (f32[6,1,8,128]{3,2,1,0:T(8,128)S(1)}, f32[6,1,8,128]{3,2,1,0:T(8,128)S(1)}, u32[]{:S(2)}, u32[]{:S(2)}) collective-permute-start(f32[6,1,8,128]{3,2,1,0:T(8,128)S(1)} %get-tuple-element.191), channel_id=1, source_target_pairs={{0,8},{8,16},{16,24},{1,9},{9,17},{17,25},{2,10},{10,18},{18,26},{... | collective-permute-start | bytes 73736 | tf_op jit(solution)/shard_map/ppermute | solution.py:16
  50.8 22.7 %collective-permute-start.1 = (f32[6,1,8,128]{3,2,1,0:T(8,128)S(1)}, f32[6,1,8,128]{3,2,1,0:T(8,128)S(1)}, u32[]{:S(2)}, u32[]{:S(2)}) collective-permute-start(f32[6,1,8,128]{3,2,1,0:T(8,128)S(1)} %get-tuple-element.192), channel_id=1, source_target_pairs={{8,0},{16,8},{24,16},{9,1},{17,9},{25,17},{10,2},{18,10},{26,18},{... | collective-permute-start | bytes 73736 | tf_op jit(solution)/shard_map/ppermute | solution.py:17
  52.1 24.2 %collective-permute-start.4 = (f32[1,128]{1,0:T(1,128)S(1)}, f32[1,128]{1,0:T(1,128)S(1)}, u32[]{:S(2)}, u32[]{:S(2)}) collective-permute-start(f32[1,128]{1,0:T(1,128)S(1)} %get-tuple-element.223), channel_id=1, source_target_pairs={{0,8},{8,16},{16,24},{1,9},{9,17},{17,25},{2,10},{10,18},{18,26},{... | collective-permute-start | bytes 1544 | tf_op jit(solution)/shard_map/ppermute | solution.py:16
  56.7 4.6 copy-start.1
  56.7 19.7 %collective-permute-start.5 = (f32[1,128]{1,0:T(1,128)S(1)}, f32[1,128]{1,0:T(1,128)S(1)}, u32[]{:S(2)}, u32[]{:S(2)}) collective-permute-start(f32[1,128]{1,0:T(1,128)S(1)} %get-tuple-element.224), channel_id=1, source_target_pairs={{8,0},{16,8},{24,16},{9,1},{17,9},{25,17},{10,2},{18,10},{26,18},{... | collective-permute-start | bytes 1544 | tf_op jit(solution)/shard_map/ppermute | solution.py:17
  58.3 0.8 copy-start.5
  60.4 0.7 copy-start.4
  73.5 4.3 collective-permute-start.2
  75.0 1.3 copy-start.3
  75.0 3.6 collective-permute-start.3
  170.5 28.9 %collective-permute-start.10 = (f32[1,128]{1,0:T(1,128)S(1)}, f32[1,128]{1,0:T(1,128)S(1)}, u32[]{:S(2)}, u32[]{:S(2)}) collective-permute-start(f32[1,128]{1,0:T(1,128)S(1)} %get-tuple-element.217), channel_id=1, source_target_pairs={{0,8},{8,16},{16,24},{1,9},{9,17},{17,25},{2,10},{10,18},{18,26},{... | collective-permute-start | bytes 1544 | tf_op jit(solution)/shard_map/ppermute | solution.py:16
  174.0 25.3 %collective-permute-start.11 = (f32[1,128]{1,0:T(1,128)S(1)}, f32[1,128]{1,0:T(1,128)S(1)}, u32[]{:S(2)}, u32[]{:S(2)}) collective-permute-start(f32[1,128]{1,0:T(1,128)S(1)} %get-tuple-element.218), channel_id=1, source_target_pairs={{8,0},{16,8},{24,16},{9,1},{17,9},{25,17},{10,2},{18,10},{26,18},{... | collective-permute-start | bytes 1544 | tf_op jit(solution)/shard_map/ppermute | solution.py:17
  175.6 20.1 %collective-permute-start.6 = (f32[6,1,8,128]{3,2,1,0:T(8,128)S(1)}, f32[6,1,8,128]{3,2,1,0:T(8,128)S(1)}, u32[]{:S(2)}, u32[]{:S(2)}) collective-permute-start(f32[6,1,8,128]{3,2,1,0:T(8,128)S(1)} %get-tuple-element.179), channel_id=1, source_target_pairs={{0,8},{8,16},{16,24},{1,9},{9,17},{17,25},{2,10},{10,18},{18,26},{... | collective-permute-start | bytes 73736 | tf_op jit(solution)/shard_map/ppermute | solution.py:16
  180.2 15.6 %collective-permute-start.7 = (f32[6,1,8,128]{3,2,1,0:T(8,128)S(1)}, f32[6,1,8,128]{3,2,1,0:T(8,128)S(1)}, u32[]{:S(2)}, u32[]{:S(2)}) collective-permute-start(f32[6,1,8,128]{3,2,1,0:T(8,128)S(1)} %get-tuple-element.180), channel_id=1, source_target_pairs={{8,0},{16,8},{24,16},{9,1},{17,9},{25,17},{10,2},{18,10},{26,18},{... | collective-permute-start | bytes 73736 | tf_op jit(solution)/shard_map/ppermute | solution.py:17
  195.8 5.6 collective-permute-start.8
  198.0 3.3 collective-permute-start.9
  294.5 25.5 %collective-permute-start.12 = (f32[6,1,8,128]{3,2,1,0:T(8,128)S(1)}, f32[6,1,8,128]{3,2,1,0:T(8,128)S(1)}, u32[]{:S(2)}, u32[]{:S(2)}) collective-permute-start(f32[6,1,8,128]{3,2,1,0:T(8,128)S(1)} %get-tuple-element.173), channel_id=1, source_target_pairs={{0,8},{8,16},{16,24},{1,9},{9,17},{17,25},{2,10},{10,18},{18,26},{... | collective-permute-start | bytes 73736 | tf_op jit(solution)/shard_map/ppermute | solution.py:16
  298.1 21.9 %collective-permute-start.13 = (f32[6,1,8,128]{3,2,1,0:T(8,128)S(1)}, f32[6,1,8,128]{3,2,1,0:T(8,128)S(1)}, u32[]{:S(2)}, u32[]{:S(2)}) collective-permute-start(f32[6,1,8,128]{3,2,1,0:T(8,128)S(1)} %get-tuple-element.174), channel_id=1, source_target_pairs={{8,0},{16,8},{24,16},{9,1},{17,9},{25,17},{10,2},{18,10},{26,18},{... | collective-permute-start | bytes 73736 | tf_op jit(solution)/shard_map/ppermute | solution.py:17
  302.1 21.0 %collective-permute-start.16 = (f32[1,128]{1,0:T(1,128)S(1)}, f32[1,128]{1,0:T(1,128)S(1)}, u32[]{:S(2)}, u32[]{:S(2)}) collective-permute-start(f32[1,128]{1,0:T(1,128)S(1)} %get-tuple-element.211), channel_id=1, source_target_pairs={{0,8},{8,16},{16,24},{1,9},{9,17},{17,25},{2,10},{10,18},{18,26},{... | collective-permute-start | bytes 1544 | tf_op jit(solution)/shard_map/ppermute | solution.py:16
  306.6 16.4 %collective-permute-start.17 = (f32[1,128]{1,0:T(1,128)S(1)}, f32[1,128]{1,0:T(1,128)S(1)}, u32[]{:S(2)}, u32[]{:S(2)}) collective-permute-start(f32[1,128]{1,0:T(1,128)S(1)} %get-tuple-element.212), channel_id=1, source_target_pairs={{8,0},{16,8},{24,16},{9,1},{17,9},{25,17},{10,2},{18,10},{26,18},{... | collective-permute-start | bytes 1544 | tf_op jit(solution)/shard_map/ppermute | solution.py:17
  320.0 5.7 collective-permute-start.14
  321.7 4.0 collective-permute-start.15
  423.3 27.5 %collective-permute-start.22 = (f32[1,128]{1,0:T(1,128)S(1)}, f32[1,128]{1,0:T(1,128)S(1)}, u32[]{:S(2)}, u32[]{:S(2)}) collective-permute-start(f32[1,128]{1,0:T(1,128)S(1)} %get-tuple-element.205), channel_id=1, source_target_pairs={{0,8},{8,16},{16,24},{1,9},{9,17},{17,25},{2,10},{10,18},{18,26},{... | collective-permute-start | bytes 1544 | tf_op jit(solution)/shard_map/ppermute | solution.py:16
  427.0 23.9 %collective-permute-start.23 = (f32[1,128]{1,0:T(1,128)S(1)}, f32[1,128]{1,0:T(1,128)S(1)}, u32[]{:S(2)}, u32[]{:S(2)}) collective-permute-start(f32[1,128]{1,0:T(1,128)S(1)} %get-tuple-element.206), channel_id=1, source_target_pairs={{8,0},{16,8},{24,16},{9,1},{17,9},{25,17},{10,2},{18,10},{26,18},{... | collective-permute-start | bytes 1544 | tf_op jit(solution)/shard_map/ppermute | solution.py:17
  428.6 19.5 %collective-permute-start.18 = (f32[6,1,8,128]{3,2,1,0:T(8,128)S(1)}, f32[6,1,8,128]{3,2,1,0:T(8,128)S(1)}, u32[]{:S(2)}, u32[]{:S(2)}) collective-permute-start(f32[6,1,8,128]{3,2,1,0:T(8,128)S(1)} %get-tuple-element.167), channel_id=1, source_target_pairs={{0,8},{8,16},{16,24},{1,9},{9,17},{17,25},{2,10},{10,18},{18,26},{... | collective-permute-start | bytes 73736 | tf_op jit(solution)/shard_map/ppermute | solution.py:16
  433.1 14.9 %collective-permute-start.19 = (f32[6,1,8,128]{3,2,1,0:T(8,128)S(1)}, f32[6,1,8,128]{3,2,1,0:T(8,128)S(1)}, u32[]{:S(2)}, u32[]{:S(2)}) collective-permute-start(f32[6,1,8,128]{3,2,1,0:T(8,128)S(1)} %get-tuple-element.168), channel_id=1, source_target_pairs={{8,0},{16,8},{24,16},{9,1},{17,9},{25,17},{10,2},{18,10},{26,18},{... | collective-permute-start | bytes 73736 | tf_op jit(solution)/shard_map/ppermute | solution.py:17
  448.1 6.1 collective-permute-start.20
  449.6 4.6 collective-permute-start.21
  554.5 28.2 %collective-permute-start.28 = (f32[1,128]{1,0:T(1,128)S(1)}, f32[1,128]{1,0:T(1,128)S(1)}, u32[]{:S(2)}, u32[]{:S(2)}) collective-permute-start(f32[1,128]{1,0:T(1,128)S(1)} %get-tuple-element.199), channel_id=1, source_target_pairs={{0,8},{8,16},{16,24},{1,9},{9,17},{17,25},{2,10},{10,18},{18,26},{... | collective-permute-start | bytes 1544 | tf_op jit(solution)/shard_map/ppermute | solution.py:16
  558.1 24.6 %collective-permute-start.29 = (f32[1,128]{1,0:T(1,128)S(1)}, f32[1,128]{1,0:T(1,128)S(1)}, u32[]{:S(2)}, u32[]{:S(2)}) collective-permute-start(f32[1,128]{1,0:T(1,128)S(1)} %get-tuple-element.200), channel_id=1, source_target_pairs={{8,0},{16,8},{24,16},{9,1},{17,9},{25,17},{10,2},{18,10},{26,18},{... | collective-permute-start | bytes 1544 | tf_op jit(solution)/shard_map/ppermute | solution.py:17
  559.7 20.1 %collective-permute-start.24 = (f32[6,1,8,128]{3,2,1,0:T(8,128)S(1)}, f32[6,1,8,128]{3,2,1,0:T(8,128)S(1)}, u32[]{:S(2)}, u32[]{:S(2)}) collective-permute-start(f32[6,1,8,128]{3,2,1,0:T(8,128)S(1)} %get-tuple-element.161), channel_id=1, source_target_pairs={{0,8},{8,16},{16,24},{1,9},{9,17},{17,25},{2,10},{10,18},{18,26},{... | collective-permute-start | bytes 73736 | tf_op jit(solution)/shard_map/ppermute | solution.py:16
  564.3 15.5 %collective-permute-start.25 = (f32[6,1,8,128]{3,2,1,0:T(8,128)S(1)}, f32[6,1,8,128]{3,2,1,0:T(8,128)S(1)}, u32[]{:S(2)}, u32[]{:S(2)}) collective-permute-start(f32[6,1,8,128]{3,2,1,0:T(8,128)S(1)} %get-tuple-element.162), channel_id=1, source_target_pairs={{8,0},{16,8},{24,16},{9,1},{17,9},{25,17},{10,2},{18,10},{26,18},{... | collective-permute-start | bytes 73736 | tf_op jit(solution)/shard_map/ppermute | solution.py:17
  579.9 6.7 collective-permute-start.26
  581.4 5.2 collective-permute-start.27
  688.9 29.4 %collective-permute-start.34 = (f32[1,128]{1,0:T(1,128)S(1)}, f32[1,128]{1,0:T(1,128)S(1)}, u32[]{:S(2)}, u32[]{:S(2)}) collective-permute-start(f32[1,128]{1,0:T(1,128)S(1)} %get-tuple-element.193), channel_id=1, source_target_pairs={{0,8},{8,16},{16,24},{1,9},{9,17},{17,25},{2,10},{10,18},{18,26},{... | collective-permute-start | bytes 1544 | tf_op jit(solution)/shard_map/ppermute | solution.py:16
  692.6 25.7 %collective-permute-start.35 = (f32[1,128]{1,0:T(1,128)S(1)}, f32[1,128]{1,0:T(1,128)S(1)}, u32[]{:S(2)}, u32[]{:S(2)}) collective-permute-start(f32[1,128]{1,0:T(1,128)S(1)} %get-tuple-element.194), channel_id=1, source_target_pairs={{8,0},{16,8},{24,16},{9,1},{17,9},{25,17},{10,2},{18,10},{26,18},{... | collective-permute-start | bytes 1544 | tf_op jit(solution)/shard_map/ppermute | solution.py:17
  694.2 21.2 %collective-permute-start.30 = (f32[6,1,8,128]{3,2,1,0:T(8,128)S(1)}, f32[6,1,8,128]{3,2,1,0:T(8,128)S(1)}, u32[]{:S(2)}, u32[]{:S(2)}) collective-permute-start(f32[6,1,8,128]{3,2,1,0:T(8,128)S(1)} %get-tuple-element.155), channel_id=1, source_target_pairs={{0,8},{8,16},{16,24},{1,9},{9,17},{17,25},{2,10},{10,18},{18,26},{... | collective-permute-start | bytes 73736 | tf_op jit(solution)/shard_map/ppermute | solution.py:16
  698.7 16.7 %collective-permute-start.31 = (f32[6,1,8,128]{3,2,1,0:T(8,128)S(1)}, f32[6,1,8,128]{3,2,1,0:T(8,128)S(1)}, u32[]{:S(2)}, u32[]{:S(2)}) collective-permute-start(f32[6,1,8,128]{3,2,1,0:T(8,128)S(1)} %get-tuple-element.156), channel_id=1, source_target_pairs={{8,0},{16,8},{24,16},{9,1},{17,9},{25,17},{10,2},{18,10},{26,18},{... | collective-permute-start | bytes 73736 | tf_op jit(solution)/shard_map/ppermute | solution.py:17
  715.4 7.4 collective-permute-start.32
  717.0 5.9 collective-permute-start.33
where the time goes:
time: 837 us; the launch traced here: 833 us
  blocking collectives  620 us (74%)
  starting transfers between devices  82.1 us (10%)
  between operations  71.4 us (9%)
  other arithmetic  49.7 us (6%)
    psum x6, blocking collectives, shards(): values = lax.psum(terms, ('span', 'flow'))  266 us
    psum x6, blocking collectives, shards(): lax.psum(local_inner((image_f, image_s), (image_f, image_s)), ('span', 'f...  239 us
    psum x6, blocking collectives, shards(): sink = lax.psum(jnp.dot(metal_pick, wall_vals, precision=highest), 'flow')  72.4 us
    ppermute x18, starting transfers between devices, extended(): before = lax.ppermute(last, axis, up)  58.7 us
    psum x1, blocking collectives, shards(): lax.psum(local_inner((rhs_fluid, rhs_solid), (rhs_fluid, rhs_solid)), ('s...  42 us
    ppermute x18, starting transfers between devices, extended(): after = lax.ppermute(first, axis, down)  23.4 us
    reduce_sum x13, other arithmetic, local_inner(): jnp.sum(left[0] * right[0]) + first_flow * jnp.sum(left[1] * right[1])  22.8 us
    reduce_sum x13, other arithmetic, local_inner(): jnp.sum(left[1] * right[1])  22.1 us
  transfers between devices with their start and end apart: 36, of which 1 were waited for; matrix products, arithmetic and copies ran while one was open for 1% of the time, Pallas kernels for 0%

commit v1 on v0

v1 whole, which is shorter than its diff:
```python
import functools
import math

import jax
import jax.numpy as jnp
from jax import lax
from jax.experimental import pallas as pl
from jax.experimental.pallas import tpu as pltpu
from jax.sharding import PartitionSpec as P

KRYLOV = 6
AXES = ("span", "flow")
F32 = jnp.float32
HI = lax.Precision.HIGHEST
PAIRS = [(i, j) for i in range(KRYLOV + 1) for j in range(i, KRYLOV + 1)]


def call(kernel, outs, *args, smem=()):
    outs = [jax.ShapeDtypeStruct(shape, F32) for shape in outs]
    moved = sum(math.prod(a.shape) for a in args) + sum(math.prod(o.shape) for o in outs)
    return pl.pallas_call(
        kernel,
        out_shape=outs,
        in_specs=[
            pl.BlockSpec(memory_space=pltpu.SMEM if n in smem else pltpu.VMEM)
            for n in range(len(args))
        ],
        out_specs=[pl.BlockSpec(memory_space=pltpu.VMEM)] * len(outs),
        cost_estimate=pl.CostEstimate(flops=8 * moved, bytes_accessed=4 * moved, transcendentals=0),
    )(*args)


def place():
    i, q = lax.axis_index("span"), lax.axis_index("flow")
    last_i, last_q = lax.axis_size("span") - 1, lax.axis_size("flow") - 1
    return (i % 2 == 1, i == 0, i == last_i), (q % 2 == 1, q == 0, q == last_q)


def iota(shape, dim):
    return lax.broadcasted_iota(jnp.int32, shape, dim)


def rows_sum(x):
    return jnp.sum(x, axis=0, keepdims=True)


def load(ref):
    return [[ref[f, a] for a in range(ref.shape[1])] for f in range(ref.shape[0])]


def store(ref, tiles):
    for f, line in enumerate(tiles):
        for a, tile in enumerate(line):
            ref[f, a] = tile


def send(tiles, flow_a, flow_b, span_a, span_b):
    (odd_i, _, _), (odd_q, _, _) = place()
    rows_a, rows_b = len(tiles[0]), tiles[0][0].shape[0]
    for f, line in enumerate(tiles):
        for a, tile in enumerate(line):
            first, last = tile[0:1], tile[rows_b - 1 : rows_b]
            row = f * rows_a + a
            flow_a[row : row + 1] = jnp.where(odd_q, first, last)
            flow_b[row : row + 1] = jnp.where(odd_q, last, first)
        span_a[f] = jnp.where(odd_i, line[0], line[-1])
        span_b[f] = jnp.where(odd_i, line[-1], line[0])


def sides(got_a, got_b, where):
    odd, first, last = where
    zero = jnp.zeros_like(got_a)
    before = jnp.where(first, zero, jnp.where(odd, got_a, got_b))
    after = jnp.where(last, zero, jnp.where(odd, got_b, got_a))
    return before, after


def receive(flow_a, flow_b, span_a, span_b, fields):
    where_i, where_q = place()
    left, right = sides(flow_a[...], flow_b[...], where_q)
    low, high = zip(*[sides(span_a[f], span_b[f], where_i) for f in range(fields)])
    return left, right, low, high


def fluid(tiles, halo, blocks, weights, inflow):
    left, right, low, high = halo
    fields, rows_a = len(tiles), len(tiles[0])
    rows_b, width = tiles[0][0].shape
    at_first = iota((rows_b, width), 0) == 0
    at_last = iota((rows_b, width), 0) == rows_b - 1
    image = [[None] * rows_a for _ in range(fields)]
    for a in range(rows_a):
        face = [weights[d, a] for d in range(6)]
        for f in range(fields):
            tile = tiles[f][a]
            row = f * rows_a + a
            local = blocks[f, 0, a] * tiles[0][a]
            for g in range(1, fields):
                local = local + blocks[f, g, a] * tiles[g][a]
            below = tiles[f][a - 1] if a else low[f]
            above = tiles[f][a + 1] if a < rows_a - 1 else high[f]
            up = jnp.where(at_first, left[row : row + 1], pltpu.roll(tile, 1, 0))
            down = jnp.where(at_last, right[row : row + 1], pltpu.roll(tile, rows_b - 1, 0))
            beside = face[0] * below + face[1] * above
            beside = beside + face[2] * up + face[3] * down
            beside = beside + face[4] * pltpu.roll(tile, 1, 1)
            beside = beside + face[5] * pltpu.roll(tile, width - 1, 1)
            out = local - beside
            if f == fields - 1:
                out = out - inflow[a]
            image[f][a] = out
    return image


def wall_row(tiles, wall):
    total = None
    for a in range(len(tiles[-1])):
        part = rows_sum(wall[a] * tiles[-1][a])
        total = part if total is None else total + part
    return total


def inflow_of(wall, row):
    return [wall[a] * row for a in range(wall.shape[0])]


def metal(u, kdiag, before=None, after=None):
    rows, width = u.shape
    at = iota(u.shape, 0)
    up = jnp.where(at == 0, 0.0 if before is None else before, pltpu.roll(u, 1, 0))
    down = jnp.where(at == rows - 1, 0.0 if after is None else after, pltpu.roll(u, rows - 1, 0))
    return (4.0 + kdiag) * u - (up + down + pltpu.roll(u, 1, 1) + pltpu.roll(u, width - 1, 1))


def shifted(image, tiles, theta, inverse):
    return [
        [(y - theta * x) * inverse for y, x in zip(ys, xs)] for ys, xs in zip(image, tiles)
    ]


def dot_rows(left, right):
    total = None
    for xs, ys in zip(left, right):
        for x, y in zip(xs, ys):
            total = x * y if total is None else total + x * y
    return rows_sum(total)


def lanes(rows, width):
    pad = -len(rows) % 8
    stack = jnp.concatenate(rows + [jnp.zeros_like(rows[0])] * pad, axis=0)
    sums = jnp.sum(stack, axis=1, keepdims=True)
    shape = (stack.shape[0], width)
    return rows_sum(jnp.where(iota(shape, 0) == iota(shape, 1), sums, 0.0))


def start_kernel(scale, patch, pair, rhs, solid, coef, w0, wall, mine, fa, fb, sa, sb):
    fields, rows_a, rows_b, width = rhs.shape
    tiles = [[t * scale for t in line] for line in load(rhs)]
    store(w0, tiles)
    send(tiles, fa, fb, sa, sb)
    (odd_i, _, _), _ = place()
    rows = solid.shape[0]
    first = jnp.broadcast_to(solid[0:1] * scale, (rows_b, width))
    last = jnp.broadcast_to(solid[rows - 1 : rows] * scale, (rows_b, width))
    sa[fields] = jnp.where(odd_i, first, last)
    sb[fields] = jnp.where(odd_i, last, first)
    for a in range(rows_a):
        hit = iota((rows_b, width), 0) + a * rows_b == patch[0, 0]
        wall[a] = jnp.where(hit, coef[...], 0.0)
    mine[...] = (iota((rows, width), 0) == pair[0, 0]).astype(F32)


def first_kernel(
    scale, w0, fa, fb, sa, sb, blocks, weights, wall, mine, solid, kdiag,
    w1, fa1, fb1, sa1, sb1, own1, packed,
):
    fields = w0.shape[0]
    where_i, _ = place()
    tiles = load(w0)
    u = solid[...] * scale
    mask = mine[...]
    own0 = rows_sum(mask * u)
    image = fluid(
        tiles, receive(fa, fb, sa, sb, fields), blocks, weights, inflow_of(wall, own0)
    )
    store(w1, image)
    send(image, fa1, fb1, sa1, sb1)
    before, after = sides(sa[fields][0:1], sb[fields][0:1], where_i)
    p0 = wall_row(tiles, wall)
    own = rows_sum(mask * metal(u, kdiag[...], before, after)) - p0
    own1[...] = own
    p1 = wall_row(image, wall)
    kd = rows_sum(mask * kdiag[...])
    rows, width = u.shape
    which = rows_sum(mask * iota(u.shape, 0).astype(F32)) + (
        lax.axis_index("span") * rows
    ).astype(F32)
    stats = lanes(
        [
            dot_rows(tiles, tiles) + own0 * own0,
            dot_rows(tiles, image) + own0 * own,
            dot_rows(image, image) + own * own,
        ],
        width,
    )
    block = jnp.concatenate(
        [p0, p1, own0, kd, which, stats, jnp.zeros((2, width), F32)], axis=0
    )
    packed[...] = jnp.broadcast_to(block[None], packed.shape)


def raw_kernel(w, fa, fb, sa, sb, blocks, weights, wall, own, out, fa1, fb1, sa1, sb1):
    tiles = load(w)
    halo = receive(fa, fb, sa, sb, w.shape[0])
    image = fluid(tiles, halo, blocks, weights, inflow_of(wall, own[...]))
    store(out, image)
    send(image, fa1, fb1, sa1, sb1)


def own_row(full, mask):
    rows = mask.shape[0]
    at = pl.multiple_of(lax.axis_index("span") * rows, rows)
    return rows_sum(mask[...] * full[pl.ds(at, rows)])


def turn(pick, slots):
    return lax.dot_general(
        pick, slots, (((0,), (0,)), ((), ())), precision=HI, preferred_element_type=F32
    )


def metal_kernel(got, mine, scal, pick, u0, u1, u2, kd, work, own2, next2):
    slots, _, width = got.shape
    at = jnp.broadcast_to(got[:, 4, :][:, 0:1], (slots, slots)).astype(jnp.int32)
    pick[...] = (at == iota((slots, slots), 1)).astype(F32)
    order = pick[...]
    stats = rows_sum(got[:, 5, :])
    norm = stats[:, 0:1]
    theta = stats[:, 1:2] / norm
    square = stats[:, 2:3] / norm - theta * theta
    sigma = jnp.where(square > 0.0, jnp.sqrt(jnp.maximum(square, 0.0)), 1.0)
    theta = jnp.broadcast_to(theta, (1, width))
    sigma = jnp.broadcast_to(sigma, (1, width))
    inverse = 1.0 / sigma
    scal[...] = jnp.concatenate([theta, inverse, sigma, jnp.zeros((5, width), F32)], axis=0)
    wall0, wall1 = turn(order, got[:, 0, :]), turn(order, got[:, 1, :])
    start, diag = turn(order, got[:, 2, :]), turn(order, got[:, 3, :])
    one = metal(start, diag) - wall0
    two = metal(one, diag) - wall1
    basis1 = (one - theta * start) * inverse
    basis2 = ((two - theta * one) * inverse - theta * basis1) * inverse
    u0[...] = start
    u1[...] = basis1
    u2[...] = basis2
    kd[...] = diag
    own2[...] = own_row(u2, mine)
    work[...] = (metal(basis2, diag) - theta * basis2) * inverse
    next2[...] = own_row(work, mine)


def third_kernel(
    w0, w1, w2, fa0, fb0, sa0, sb0, fa1, fb1, sa1, sb1, fa2, fb2, sa2, sb2,
    blocks, weights, wall, scal, own2, next2,
    b1, b2, w3, fa3, fb3, sa3, sb3, own3, packed,
):
    fields = w0.shape[0]
    theta, inverse = scal[0:1], scal[1:2]

    def recombine(x0, x1, x2):
        y1 = (x1 - theta * x0) * inverse
        return y1, ((x2 - theta * x1) * inverse - theta * y1) * inverse

    tiles1, tiles2 = [], []
    for l0, l1, l2 in zip(load(w0), load(w1), load(w2)):
        pairs = [recombine(*x) for x in zip(l0, l1, l2)]
        tiles1.append([p[0] for p in pairs])
        tiles2.append([p[1] for p in pairs])
    store(b1, tiles1)
    store(b2, tiles2)
    where_i, where_q = place()
    mix = lambda *x: recombine(*x)[1]
    left, right = sides(
        mix(fa0[...], fa1[...], fa2[...]), mix(fb0[...], fb1[...], fb2[...]), where_q
    )
    low, high = zip(*[
        sides(mix(sa0[f], sa1[f], sa2[f]), mix(sb0[f], sb1[f], sb2[f]), where_i)
        for f in range(fields)
    ])
    image = fluid(
        tiles2, (left, right, low, high), blocks, weights, inflow_of(wall, own2[...])
    )
    tiles3 = shifted(image, tiles2, theta, inverse)
    store(w3, tiles3)
    send(tiles3, fa3, fb3, sa3, sb3)
    p2, p3 = wall_row(tiles2, wall), wall_row(tiles3, wall)
    own3[...] = next2[...] - p2 * inverse
    block = jnp.concatenate([p2, p3], axis=0)
    packed[...] = jnp.broadcast_to(block[None], packed.shape)


def step_kernel(
    w, fa, fb, sa, sb, blocks, weights, wall, scal, own, out, fa1, fb1, sa1, sb1
):
    theta, inverse = scal[0:1], scal[1:2]
    tiles = load(w)
    halo = receive(fa, fb, sa, sb, w.shape[0])
    image = fluid(tiles, halo, blocks, weights, inflow_of(wall, own[...]))
    tiles = shifted(image, tiles, theta, inverse)
    store(out, tiles)
    send(tiles, fa1, fb1, sa1, sb1)


def metal_step(u, diag, wall, theta, inverse):
    return (metal(u, diag) - wall - theta * u) * inverse


def second_metal_kernel(got, pick, kd, u2, scal, mine, u3, u4, work, own4, next4):
    theta, inverse = scal[0:1], scal[1:2]
    order, diag = pick[...], kd[...]
    three = metal_step(u2[...], diag, turn(order, got[:, 0, :]), theta, inverse)
    four = metal_step(three, diag, turn(order, got[:, 1, :]), theta, inverse)
    u3[...] = three
    u4[...] = four
    own4[...] = own_row(u4, mine)
    work[...] = (metal(four, diag) - theta * four) * inverse
    next4[...] = own_row(work, mine)


def fifth_kernel(
    w, fa, fb, sa, sb, blocks, weights, wall, scal, own, following,
    out, fa1, fb1, sa1, sb1, own5,
):
    step_kernel(
        w, fa, fb, sa, sb, blocks, weights, wall, scal, own, out, fa1, fb1, sa1, sb1
    )
    own5[...] = following[...] - wall_row(load(w), wall) * scal[1:2]


def last_kernel(
    w0, w1, w2, w3, w4, w5, fa, fb, sa, sb, blocks, weights, wall, scal, own, packed
):
    theta, inverse = scal[0:1], scal[1:2]
    width = w0.shape[3]
    basis = [load(w) for w in (w0, w1, w2, w3, w4, w5)]
    halo = receive(fa, fb, sa, sb, w0.shape[0])
    image = fluid(basis[5], halo, blocks, weights, inflow_of(wall, own[...]))
    basis.append(shifted(image, basis[5], theta, inverse))
    sums = lanes([dot_rows(basis[i], basis[j]) for i, j in PAIRS], width)
    block = jnp.concatenate(
        [sums, wall_row(basis[4], wall), wall_row(basis[5], wall), jnp.zeros_like(sums)], axis=0
    )
    packed[...] = jnp.broadcast_to(block[None], packed.shape)


def solve(gram, theta, sigma):
    n = KRYLOV
    g = lambda i, j: gram[min(i, j), max(i, j)]
    mat = [[None] * n for _ in range(n)]
    vec = []
    for j in range(n):
        for k in range(j + 1):
            mat[j][k] = (
                sigma * (sigma * g(j + 1, k + 1) + theta * (g(j + 1, k) + g(j, k + 1)))
                + theta * theta * g(j, k)
            )
        vec.append(sigma * g(j + 1, 0) + theta * g(j, 0))
    inv = []
    for j in range(n):
        inv.append(1.0 / mat[j][j])
        for i in range(j + 1, n):
            factor = mat[i][j] * inv[j]
            for k in range(j + 1, i + 1):
                mat[i][k] = mat[i][k] - factor * mat[k][j]
            vec[i] = vec[i] - factor * vec[j]
    out = [None] * n
    for j in range(n - 1, -1, -1):
        total = vec[j]
        for k in range(j + 1, n):
            total = total - mat[k][j] * out[k]
        out[j] = total * inv[j]
    return out


def end_kernel(
    scale, got, pick, kd, scal, u0, u1, u2, u3, u4, w0, w1, w2, w3, w4, w5,
    x_fluid, x_solid, work,
):
    theta, inverse = scal[0:1], scal[1:2]
    width = w0.shape[3]
    order, diag = pick[...], kd[...]
    u = [r[...] for r in (u0, u1, u2, u3, u4)]
    u.append(metal_step(u[4], diag, turn(order, got[:, 1, :]), theta, inverse))
    u.append(metal_step(u[5], diag, turn(order, got[:, 2, :]), theta, inverse))
    sums = rows_sum(got[:, 0, :]) + lanes([rows_sum(u[i] * u[j]) for i, j in PAIRS], width)
    gram = {pair: sums[:, n : n + 1] for n, pair in enumerate(PAIRS)}
    coeffs = solve(gram, scal[0:1, 0:1], scal[2:3, 0:1])
    coeffs = [jnp.broadcast_to(c * (1.0 / scale), (1, width)) for c in coeffs]
    basis = (w0, w1, w2, w3, w4, w5)
    for f in range(w0.shape[0]):
        for a in range(w0.shape[1]):
            total = coeffs[0] * w0[f, a]
            for j in range(1, KRYLOV):
                total = total + coeffs[j] * basis[j][f, a]
            x_fluid[f, a] = total
    total = coeffs[0] * u[0]
    for j in range(1, KRYLOV):
        total = total + coeffs[j] * u[j]
    work[...] = total
    rows = x_solid.shape[0]
    at = pl.multiple_of(lax.axis_index("span") * rows, rows)
    x_solid[...] = work[pl.ds(at, rows)]


def pairings(n_span, n_flow):
    even = lambda n: [(i, i ^ 1) for i in range(n)]
    odd = lambda n: [(i, (i + 1) % n if i % 2 else (i - 1) % n) for i in range(n)]
    both = []
    for i in range(n_span):
        for q in range(n_flow):
            other = i + 1 if i % 2 else i - 1
            to = (other, q) if 0 <= other < n_span else (i, q ^ 1)
            both.append((i * n_flow + q, to[0] * n_flow + to[1]))
    return even(n_flow), odd(n_flow), even(n_span), both


def shards(rhs_fluid, rhs_solid, blocks, weights, kdiag, wall_fluid, wall_solid, wall_coef):
    n_span, n_flow = lax.axis_size("span"), lax.axis_size("flow")
    fields, rows_a, rows_b, width = rhs_fluid.shape
    rows = rhs_solid.shape[0]
    devices = n_span * n_flow
    count = fields * rows_a * rows_b * width * devices + rows * width * n_span
    scale = 2.0 ** -math.ceil(math.log2(6.0 * math.sqrt(count)))
    flow_a, flow_b, span_a, span_b = pairings(n_span, n_flow)

    def exchange(fa, fb, sa, sb):
        return (
            lax.ppermute(fa, "flow", flow_a),
            lax.ppermute(fb, "flow", flow_b),
            lax.ppermute(sa, "span", span_a),
            lax.ppermute(sb, AXES, span_b),
        )

    def gather(packed):
        return lax.all_to_all(packed, AXES, 0, 0)

    tile = rhs_fluid.shape
    row = (1, width)
    full = (devices, width)
    edges = [(fields * rows_a, width)] * 2 + [(fields, rows_b, width)] * 2
    edges0 = edges[:2] + [(fields + 1, rows_b, width)] * 2

    w0, wall, mine, *out = call(
        functools.partial(start_kernel, scale),
        [tile, (rows_a, rows_b, width), (rows, width)] + edges0,
        wall_fluid, wall_solid, rhs_fluid, rhs_solid, wall_coef[0],
        smem=(0, 1),
    )
    halo0 = exchange(*out)
    w1, *out, own1, packed = call(
        functools.partial(first_kernel, scale),
        [tile] + edges + [row, (devices, 8, width)],
        w0, *halo0, blocks, weights, wall, mine, rhs_solid, kdiag,
    )
    halo1 = exchange(*out)
    got = gather(packed)
    w2, *out = call(raw_kernel, [tile] + edges, w1, *halo1, blocks, weights, wall, own1)
    halo2 = exchange(*out)
    scal, pick, u0, u1, u2, kd, _, own2, next2 = call(
        metal_kernel,
        [(8, width), (devices, devices)] + [full] * 5 + [row, row],
        got, mine,
    )
    b1, b2, w3, *out, own3, packed = call(
        third_kernel,
        [tile] * 3 + edges + [row, (devices, 2, width)],
        w0, w1, w2, *halo0, *halo1, *halo2, blocks, weights, wall, scal, own2, next2,
    )
    halo3 = exchange(*out)
    got = gather(packed)
    w4, *out = call(
        step_kernel, [tile] + edges, w3, *halo3, blocks, weights, wall, scal, own3
    )
    halo4 = exchange(*out)
    u3, u4, _, own4, next4 = call(
        second_metal_kernel, [full] * 3 + [row, row], got, pick, kd, u2, scal, mine
    )
    w5, *out, own5 = call(
        fifth_kernel,
        [tile] + edges + [row],
        w4, *halo4, blocks, weights, wall, scal, own4, next4,
    )
    halo5 = exchange(*out)
    (packed,) = call(
        last_kernel,
        [(devices, 4, width)],
        w0, b1, b2, w3, w4, w5, *halo5, blocks, weights, wall, scal, own5,
    )
    got = gather(packed)
    x_fluid, x_solid, _ = call(
        functools.partial(end_kernel, scale),
        [tile, (rows, width), full],
        got, pick, kd, scal, u0, u1, u2, u3, u4, w0, b1, b2, w3, w4, w5,
    )
    return x_fluid, x_solid


def solution(mesh):
    in_specs = (
        P(None, "span", "flow", None),
        P("span", None),
        P(None, None, "span", "flow", None),
        P(None, "span", "flow", None),
        P("span", None),
        P("span", "flow"),
        P("span", "flow"),
        P("span", "flow", None),
    )
    out_specs = (P(None, "span", "flow", None), P("span", None))
    return jax.shard_map(shards, mesh=mesh, in_specs=in_specs, out_specs=out_specs, check_vma=False)
```

time: 837 us -> 81.6 us (0.10)
  blocking collectives: 620 us -> 11.4 us
  between operations: 71.4 us -> 2.26 us
  other arithmetic: 49.7 us -> 0 us
  starting transfers between devices: 82.1 us -> 34.9 us
  Pallas kernels: 0 us -> 18.9 us
    psum x19 -> x0, blocking collectives: 620 us -> none  [the longest x6 266 us: shards(): values = lax.psum(terms, ('span', 'flow'))]
    ppermute x36 -> x24, starting transfers between devices: 82.1 us -> 27.2 us  [the longest x6 12.3 us: exchange(): lax.ppermute(fb, 'flow', flow_b)]
    reduce_sum x26 -> x0, other arithmetic: 44.9 us -> none  [the longest x13 22.8 us: local_inner(): jnp.sum(left[0] * right[0]) + first_flow * jnp.sum(left[1] * right[1])]
    pallas_call x0 -> x10, Pallas kernels: none -> 18.9 us  [call(): pl.pallas_call(kernel, out_shape=outs, in_specs=[pl.BlockSpec(memory_spac...]
    all_to_all x0 -> x1, blocking collectives: none -> 11.4 us  [gather(): return lax.all_to_all(packed, AXES, 0, 0)]
  transfers between devices with their start and end apart: 36 -> 26, of which waited for: 1 -> 4; matrix products, arithmetic and copies ran while one was open for 1% -> 0% of each run, Pallas kernels for 0% -> 9%
where the time goes in v1:
time: 81.6 us; the launch traced here: 80.9 us
  starting transfers between devices  34.9 us (43%)
  Pallas kernels  18.9 us (23%)
  blocking collectives  11.4 us (14%)
  waiting for transfers between devices  8.47 us (10%)
  local copies, waits for them, and re-layouts  4.92 us (6%)
  between operations  2.26 us (3%)
    pallas_call x10, Pallas kernels, call(): pl.pallas_call(kernel, out_shape=outs, in_specs=[pl.BlockSpec(memory_spac...  18.9 us
    ppermute x6, starting transfers between devices, exchange(): lax.ppermute(fb, 'flow', flow_b)  12.3 us
    ppermute x6, starting transfers between devices, exchange(): lax.ppermute(sa, 'span', span_a)  11.8 us
    all_to_all x1, blocking collectives, gather(): return lax.all_to_all(packed, AXES, 0, 0)  11.4 us
    ppermute x6, waiting for transfers between devices, exchange(): lax.ppermute(fb, 'flow', flow_b)  8.42 us
    all_to_all x2, starting transfers between devices, gather(): return lax.all_to_all(packed, AXES, 0, 0)  7.72 us
    unnamed x68, local copies, waits for them, and re-layouts  4.92 us
    ppermute x6, starting transfers between devices, exchange(): lax.ppermute(fa, 'flow', flow_a)  3.03 us
  transfers between devices with their start and end apart: 26, of which 4 were waited for; matrix products, arithmetic and copies ran while one was open for 0% of the time, Pallas kernels for 9%

profile of v1, /device:TPU:0, one launch (start us, length us, event | category | flops | bytes accessed | tf_op | source)
XLA Modules:
  0.0 80.9 jit_solution(15160492228564497518)
XLA Ops:
  1.9 1.5 %shard_map.95 = (f32[6,2,8,128]{3,2,1,0:T(8,128)}, f32[2,8,128]{2,1,0:T(8,128)}, f32[8,128]{1,0:T(8,128)}, f32[12,128]{1,0:T(8,128)}, f32[12,128]{1,0:T(8,128)},...) custom-call(s32[1,1]{1,0:T(1,128)S(6)} %copy.10.patch, s32[1,1]{1,0:T(1,128)S(6)} %copy.11.pair, f32[6,2,8,128]{3,2,1,0:T(8,128)} %rhs.1, ...), custom_call_target="tpu_custom_call" | custom-call | flops 369680 | bytes 184840 | tf_op jit(solution)/shard_map/pallas_call | solution.py:21
  3.4 3.1 %collective-permute-start.2 = (f32[7,8,128]{2,1,0:T(8,128)}, f32[7,8,128]{2,1,0:T(8,128)S(1)}, u32[]{:S(2)}, u32[]{:S(2)}) collective-permute-start(f32[7,8,128]{2,1,0:T(8,128)} %get-tuple-element.58), channel_id=1, source_target_pairs={{0,8},{8,0},{16,24},{24,16},{1,9},{9,1},{17,25},{25,17},{2,10},{10... | collective-permute-start | bytes 86024 | tf_op jit(solution)/shard_map/ppermute | solution.py:440
  6.5 0.5 collective-permute-start
  7.0 2.1 %collective-permute-start.1 = (f32[12,128]{1,0:T(8,128)}, f32[12,128]{1,0:T(8,128)S(1)}, u32[]{:S(2)}, u32[]{:S(2)}) collective-permute-start(f32[12,128]{1,0:T(8,128)} %get-tuple-element.57), channel_id=1, source_target_pairs={{0,7},{1,2},{2,1},{3,4},{4,3},{5,6},{6,5},{7,0},{8,15},{9,10},{10,... | collective-permute-start | bytes 18440 | tf_op jit(solution)/shard_map/ppermute | solution.py:439
  9.0 2.1 %collective-permute-done.1.fb.fb0 = f32[12,128]{1,0:T(8,128)S(1)} collective-permute-done((f32[12,128]{1,0:T(8,128)}, f32[12,128]{1,0:T(8,128)S(1)}, u32[]{:S(2)}, u32[]{:S(2)}) %collective-permute-start.1) | collective-permute-done | bytes 6176 | tf_op jit(solution)/shard_map/ppermute | solution.py:439
  11.2 0.6 copy-done.7
  11.8 1.9 %shard_map.96 = (f32[6,2,8,128]{3,2,1,0:T(8,128)}, f32[12,128]{1,0:T(8,128)}, f32[12,128]{1,0:T(8,128)}, f32[6,8,128]{2,1,0:T(8,128)}, f32[6,8,128]{2,1,0:T(8,12...) custom-call(f32[6,2,8,128]{3,2,1,0:T(8,128)} %get-tuple-element.55.w0, f32[12,128]{1,0:T(8,128)} %copy-done.6, ...), custom_call_target="tpu_custom_call" | custom-call | flops 1451008 | bytes 725504 | tf_op jit(solution)/shard_map/pallas_call | solution.py:21
  13.7 5.0 %all-to-all-start = ((f32[32,8,128]{2,1,0:T(8,128)}), f32[32,8,128]{2,1,0:T(8,128)S(1)}, u32[]{:S(2)}, u32[]{:S(2)}) async-start(f32[32,8,128]{2,1,0:T(8,128)} %get-tuple-element.73), calls=%async_computation | async-start | bytes 262144 | tf_op jit(solution)/shard_map/all_to_all | solution.py:445
  18.7 1.8 %collective-permute-start.6 = (f32[6,8,128]{2,1,0:T(8,128)S(1)}, f32[6,8,128]{2,1,0:T(8,128)S(1)}, u32[]{:S(2)}, u32[]{:S(2)}) collective-permute-start(f32[6,8,128]{2,1,0:T(8,128)S(1)} %copy-done.29), channel_id=1, source_target_pairs={{0,8},{8,0},{16,24},{24,16},{1,9},{9,1},{17,25},{25,17},{2,10},{10... | collective-permute-start | bytes 73736 | tf_op jit(solution)/shard_map/ppermute | solution.py:440
  20.6 0.5 collective-permute-start.4
  21.1 2.0 %collective-permute-start.5 = (f32[12,128]{1,0:T(8,128)S(1)}, f32[12,128]{1,0:T(8,128)S(1)}, u32[]{:S(2)}, u32[]{:S(2)}) collective-permute-start(f32[12,128]{1,0:T(8,128)S(1)} %copy-done.32), channel_id=1, source_target_pairs={{0,7},{1,2},{2,1},{3,4},{4,3},{5,6},{6,5},{7,0},{8,15},{9,10},{10,... | collective-permute-start | bytes 18440 | tf_op jit(solution)/shard_map/ppermute | solution.py:439
  23.1 1.9 %collective-permute-done.5.fb.fb1 = f32[12,128]{1,0:T(8,128)S(1)} collective-permute-done((f32[12,128]{1,0:T(8,128)S(1)}, f32[12,128]{1,0:T(8,128)S(1)}, u32[]{:S(2)}, u32[]{:S(2)}) %collective-permute-start.5) | collective-permute-done | bytes 6176 | tf_op jit(solution)/shard_map/ppermute | solution.py:439
  25.1 0.6 copy-done.9
  25.7 1.8 %shard_map.97 = (f32[6,2,8,128]{3,2,1,0:T(8,128)}, f32[12,128]{1,0:T(8,128)}, f32[12,128]{1,0:T(8,128)}, f32[6,8,128]{2,1,0:T(8,128)}, f32[6,8,128]{2,1,0:T(8,128)}) custom-call(f32[6,2,8,128]{3,2,1,0:T(8,128)} %get-tuple-element.62.w.w1, f32[12,128]{1,0:T(8,128)} %copy-done.8, f32[12,128]{1,0:T(8,128)} %copy-done.9, f32[6,8,128]{2,1,0:T(8,128)} %copy-done.4, ...), custom_call_target="tpu_custom_call" | custom-call | flops 1147904 | bytes 573952 | tf_op jit(solution)/shard_map/pallas_call | solution.py:21
  27.4 2.5 %collective-permute-start.10 = (f32[6,8,128]{2,1,0:T(8,128)}, f32[6,8,128]{2,1,0:T(8,128)S(1)}, u32[]{:S(2)}, u32[]{:S(2)}) collective-permute-start(f32[6,8,128]{2,1,0:T(8,128)} %get-tuple-element.71), channel_id=1, source_target_pairs={{0,8},{8,0},{16,24},{24,16},{1,9},{9,1},{17,25},{25,17},{2,10},{10... | collective-permute-start | bytes 73736 | tf_op jit(solution)/shard_map/ppermute | solution.py:440
  30.0 0.5 collective-permute-start.8
  30.5 2.2 %collective-permute-start.9 = (f32[12,128]{1,0:T(8,128)}, f32[12,128]{1,0:T(8,128)S(1)}, u32[]{:S(2)}, u32[]{:S(2)}) collective-permute-start(f32[12,128]{1,0:T(8,128)} %get-tuple-element.70), channel_id=1, source_target_pairs={{0,7},{1,2},{2,1},{3,4},{4,3},{5,6},{6,5},{7,0},{8,15},{9,10},{10,... | collective-permute-start | bytes 18440 | tf_op jit(solution)/shard_map/ppermute | solution.py:439
  32.7 0.7 copy-done
  33.3 2.1 %shard_map.98 = (f32[8,128]{1,0:T(8,128)}, f32[32,32]{1,0:T(8,128)}, f32[32,128]{1,0:T(8,128)}, f32[32,128]{1,0:T(8,128)}, f32[32,128]{1,0:T(8,128)}, /*index=5*...) custom-call(f32[32,8,128]{2,1,0:T(8,128)} %copy-done, f32[8,128]{1,0:T(8,128)} %get-tuple-element.61.mine), custom_call_target="tpu_custom_call" | custom-call | flops 452608 | bytes 226304 | tf_op jit(solution)/shard_map/pallas_call | solution.py:21
  35.5 0.5 copy-done.18
  36.1 0.0 copy-done.10
  36.1 0.0 copy-done.11
  36.1 1.9 %shard_map.99 = (f32[6,2,8,128]{3,2,1,0:T(8,128)}, f32[6,2,8,128]{3,2,1,0:T(8,128)}, f32[6,2,8,128]{3,2,1,0:T(8,128)}, f32[12,128]{1,0:T(8,128)}, f32[12,128]{1,...) custom-call(f32[6,2,8,128]{3,2,1,0:T(8,128)} %get-tuple-element.55.w0, ...), custom_call_target="tpu_custom_call" | custom-call | flops 1879040 | bytes 939520 | tf_op jit(solution)/shard_map/pallas_call | solution.py:21
  38.1 2.7 %all-to-all-start.1 = ((f32[32,2,128]{2,1,0:T(2,128)}), f32[32,2,128]{2,1,0:T(2,128)S(1)}, u32[]{:S(2)}, u32[]{:S(2)}) async-start(f32[32,2,128]{2,1,0:T(2,128)} %get-tuple-element.90), calls=%async_computation.1 | async-start | bytes 65536 | tf_op jit(solution)/shard_map/all_to_all | solution.py:445
  40.8 1.8 %collective-permute-start.14 = (f32[6,8,128]{2,1,0:T(8,128)S(1)}, f32[6,8,128]{2,1,0:T(8,128)S(1)}, u32[]{:S(2)}, u32[]{:S(2)}) collective-permute-start(f32[6,8,128]{2,1,0:T(8,128)S(1)} %copy-done.27), channel_id=1, source_target_pairs={{0,8},{8,0},{16,24},{24,16},{1,9},{9,1},{17,25},{25,17},{2,10},{10... | collective-permute-start | bytes 73736 | tf_op jit(solution)/shard_map/ppermute | solution.py:440
  42.6 0.5 collective-permute-start.12
  43.1 2.1 %collective-permute-start.13 = (f32[12,128]{1,0:T(8,128)S(1)}, f32[12,128]{1,0:T(8,128)S(1)}, u32[]{:S(2)}, u32[]{:S(2)}) collective-permute-start(f32[12,128]{1,0:T(8,128)S(1)} %copy-done.30), channel_id=1, source_target_pairs={{0,7},{1,2},{2,1},{3,4},{4,3},{5,6},{6,5},{7,0},{8,15},{9,10},{10,... | collective-permute-start | bytes 18440 | tf_op jit(solution)/shard_map/ppermute | solution.py:439
  45.2 1.9 %collective-permute-done.13.fb = f32[12,128]{1,0:T(8,128)S(1)} collective-permute-done((f32[12,128]{1,0:T(8,128)S(1)}, f32[12,128]{1,0:T(8,128)S(1)}, u32[]{:S(2)}, u32[]{:S(2)}) %collective-permute-start.13) | collective-permute-done | bytes 6176 | tf_op jit(solution)/shard_map/ppermute | solution.py:439
  47.1 0.6 copy-done.24
  47.7 1.8 %shard_map.100 = (f32[6,2,8,128]{3,2,1,0:T(8,128)}, f32[12,128]{1,0:T(8,128)}, f32[12,128]{1,0:T(8,128)}, f32[6,8,128]{2,1,0:T(8,128)}, f32[6,8,128]{2,1,0:T(8,128)}) custom-call(f32[6,2,8,128]{3,2,1,0:T(8,128)} %get-tuple-element.79.w.w3, f32[12,128]{1,0:T(8,128)} %copy-done.22, f32[12,128]{1,0:T(8,128)} %copy-done.24, f32[6,8,128]{2,1,0:T(8,128)} %copy-done.14, ...), custom_call_target="tpu_custom_call" | custom-call | flops 1156096 | bytes 578048 | tf_op jit(solution)/shard_map/pallas_call | solution.py:21
  49.4 2.6 %collective-permute-start.18 = (f32[6,8,128]{2,1,0:T(8,128)}, f32[6,8,128]{2,1,0:T(8,128)S(1)}, u32[]{:S(2)}, u32[]{:S(2)}) collective-permute-start(f32[6,8,128]{2,1,0:T(8,128)} %get-tuple-element.88), channel_id=1, source_target_pairs={{0,8},{8,0},{16,24},{24,16},{1,9},{9,1},{17,25},{25,17},{2,10},{10... | collective-permute-start | bytes 73736 | tf_op jit(solution)/shard_map/ppermute | solution.py:440
  52.1 0.5 collective-permute-start.16
  52.6 2.2 %collective-permute-start.17 = (f32[12,128]{1,0:T(8,128)}, f32[12,128]{1,0:T(8,128)S(1)}, u32[]{:S(2)}, u32[]{:S(2)}) collective-permute-start(f32[12,128]{1,0:T(8,128)} %get-tuple-element.87), channel_id=1, source_target_pairs={{0,7},{1,2},{2,1},{3,4},{4,3},{5,6},{6,5},{7,0},{8,15},{9,10},{10,... | collective-permute-start | bytes 18440 | tf_op jit(solution)/shard_map/ppermute | solution.py:439
  54.7 0.6 copy-done.1
  55.4 1.8 %shard_map.101 = (f32[32,128]{1,0:T(8,128)}, f32[32,128]{1,0:T(8,128)}, f32[32,128]{1,0:T(8,128)}, f32[1,128]{1,0:T(1,128)}, f32[1,128]{1,0:T(1,128)}) custom-call(f32[32,2,128]{2,1,0:T(2,128)} %copy-done.1, f32[32,32]{1,0:T(8,128)} %get-tuple-element.91.pick, f32[32,128]{1,0:T(8,128)} %get-tuple-element.92.kd, f32[32,128]{1,0:T(8,128)} %get-tuple-element.93.u2, ...), custom_call_target="tpu_custom_call" | custom-call | flops 256000 | bytes 128000 | tf_op jit(solution)/shard_map/pallas_call | solution.py:21
  57.2 0.5 copy-done.20
  57.8 0.0 copy-done.12
  57.8 0.0 copy-done.13
  57.8 1.7 %shard_map.102 = (f32[6,2,8,128]{3,2,1,0:T(8,128)}, f32[12,128]{1,0:T(8,128)}, f32[12,128]{1,0:T(8,128)}, f32[6,8,128]{2,1,0:T(8,128)}, f32[6,8,128]{2,1,0:T(8,128)}, /*index=5*/f32[1,128]{1,0:T(1,128)}) custom-call(f32[6,2,8,128]{3,2,1,0:T(8,128)} %get-tuple-element.85.w.w4, f32[12,128]{1,0:T(8,128)} %copy-done.20, f32[12,128]{1,0:T(8,128)} %copy-done.21, ...), custom_call_target="tpu_custom_call" | custom-call | flops 1158144 | bytes 579072 | tf_op jit(solution)/shard_map/pallas_call | solution.py:21
  59.6 0.1 collective-permute-start.22
  59.6 0.1 collective-permute-start.23
  59.7 0.5 collective-permute-start.20
  60.2 1.7 %collective-permute-start.21 = (f32[12,128]{1,0:T(8,128)}, f32[12,128]{1,0:T(8,128)S(1)}, u32[]{:S(2)}, u32[]{:S(2)}) collective-permute-start(f32[12,128]{1,0:T(8,128)} %get-tuple-element.98), channel_id=1, source_target_pairs={{0,7},{1,2},{2,1},{3,4},{4,3},{5,6},{6,5},{7,0},{8,15},{9,10},{10,... | collective-permute-start | bytes 18440 | tf_op jit(solution)/shard_map/ppermute | solution.py:439
  61.9 2.5 %collective-permute-done.21.fb = f32[12,128]{1,0:T(8,128)S(1)} collective-permute-done((f32[12,128]{1,0:T(8,128)}, f32[12,128]{1,0:T(8,128)S(1)}, u32[]{:S(2)}, u32[]{:S(2)}) %collective-permute-start.21) | collective-permute-done | bytes 6176 | tf_op jit(solution)/shard_map/ppermute | solution.py:439
  64.4 0.6 copy-done.25
  65.0 2.1 %shard_map.103 = f32[32,4,128]{2,1,0:T(4,128)} custom-call(f32[6,2,8,128]{3,2,1,0:T(8,128)} %get-tuple-element.55.w0, f32[6,2,8,128]{3,2,1,0:T(8,128)} %get-tuple-element.77.w1, f32[6,2,8,128]{3,2,1,0:T(8,128)} %get-tuple-element.78.w2, f32[6,2,8,128]{3,2,1,0:T(8,128)} %get-tuple-element.79.w.w3, f32[6,2,8,128]{3,2,1,0:T(8,128)} %get-tuple-element.85.w.w4, ...), custom_call_target="tpu_custom_call" | custom-call | flops 1557504 | bytes 778752 | tf_op jit(solution)/shard_map/pallas_call | solution.py:21
  67.1 11.4 %all_to_all.15.got = f32[32,4,128]{2,1,0:T(4,128)} all-to-all(f32[32,4,128]{2,1,0:T(4,128)} %shard_map.103), channel_id=1, replica_groups=mesh['span'=4,'flow'=8] {'span','flow'}, dimensions={0} | all-to-all | bytes 131072 | tf_op jit(solution)/shard_map/all_to_all | solution.py:445
  78.5 2.4 %shard_map.104 = (f32[6,2,8,128]{3,2,1,0:T(8,128)}, f32[8,128]{1,0:T(8,128)}, f32[32,128]{1,0:T(8,128)}) custom-call(f32[32,4,128]{2,1,0:T(4,128)} %all_to_all.15.got, f32[32,32]{1,0:T(8,128)} %get-tuple-element.91.pick, f32[32,128]{1,0:T(8,128)} %get-tuple-element.92.kd, f32[8,128]{1,0:T(8,128)} %get-tuple-element.74.scal, ...), custom_call_target="tpu_custom_call" | custom-call | flops 1073152 | bytes 536576 | tf_op jit(solution)/shard_map/pallas_call | solution.py:21
  (83 shorter events, 0.3 us)
Async XLA Ops:
  3.4 7.8 %collective-permute-start.2 = (f32[7,8,128]{2,1,0:T(8,128)}, f32[7,8,128]{2,1,0:T(8,128)S(1)}, u32[]{:S(2)}, u32[]{:S(2)}) collective-permute-start(f32[7,8,128]{2,1,0:T(8,128)} %get-tuple-element.58), channel_id=1, source_target_pairs={{0,8},{8,0},{16,24},{24,16},{1,9},{9,1},{17,25},{25,17},{2,10},{10... | collective-permute-start | bytes 86024 | tf_op jit(solution)/shard_map/ppermute | solution.py:440
  6.5 4.7 %collective-permute-start.3 = (f32[7,8,128]{2,1,0:T(8,128)}, f32[7,8,128]{2,1,0:T(8,128)S(1)}, u32[]{:S(2)}, u32[]{:S(2)}) collective-permute-start(f32[7,8,128]{2,1,0:T(8,128)} %get-tuple-element.59), channel_id=1, source_target_pairs={{0,1},{1,0},{2,3},{3,2},{4,5},{5,4},{6,7},{7,6},{8,16},{9,17},{10,... | collective-permute-start | bytes 86024 | tf_op jit(solution)/shard_map/ppermute | solution.py:441
  6.5 2.6 %collective-permute-start = (f32[12,128]{1,0:T(8,128)}, f32[12,128]{1,0:T(8,128)S(1)}, u32[]{:S(2)}, u32[]{:S(2)}) collective-permute-start(f32[12,128]{1,0:T(8,128)} %get-tuple-element.56), channel_id=1, source_target_pairs={{0,1},{1,0},{2,3},{3,2},{4,5},{5,4},{6,7},{7,6},{8,9},{9,8},{10,11... | collective-permute-start | bytes 18440 | tf_op jit(solution)/shard_map/ppermute | solution.py:438
  7.0 4.2 %collective-permute-start.1 = (f32[12,128]{1,0:T(8,128)}, f32[12,128]{1,0:T(8,128)S(1)}, u32[]{:S(2)}, u32[]{:S(2)}) collective-permute-start(f32[12,128]{1,0:T(8,128)} %get-tuple-element.57), channel_id=1, source_target_pairs={{0,7},{1,2},{2,1},{3,4},{4,3},{5,6},{6,5},{7,0},{8,15},{9,10},{10,... | collective-permute-start | bytes 18440 | tf_op jit(solution)/shard_map/ppermute | solution.py:439
  9.0 2.2 %copy-start.6 = (f32[12,128]{1,0:T(8,128)}, f32[12,128]{1,0:T(8,128)S(1)}, u32[]{:S(2)}) copy-start(f32[12,128]{1,0:T(8,128)S(1)} %collective-permute-done.fa.fa0) | copy-start | bytes 18436
  11.2 0.6 copy-start.3
  13.7 5.0 %copy-start.29 = (f32[6,8,128]{2,1,0:T(8,128)S(1)}, f32[6,8,128]{2,1,0:T(8,128)}, u32[]{:S(2)}) copy-start(f32[6,8,128]{2,1,0:T(8,128)} %get-tuple-element.65) | copy-start | bytes 73732
  13.7 6.9 %copy-start.28 = (f32[6,8,128]{2,1,0:T(8,128)S(1)}, f32[6,8,128]{2,1,0:T(8,128)}, u32[]{:S(2)}) copy-start(f32[6,8,128]{2,1,0:T(8,128)} %get-tuple-element.66) | copy-start | bytes 73732
  13.7 6.9 %copy-start.33 = (f32[12,128]{1,0:T(8,128)S(1)}, f32[12,128]{1,0:T(8,128)}, u32[]{:S(2)}) copy-start(f32[12,128]{1,0:T(8,128)} %get-tuple-element.63) | copy-start | bytes 18436
  13.7 7.4 %copy-start.32 = (f32[12,128]{1,0:T(8,128)S(1)}, f32[12,128]{1,0:T(8,128)}, u32[]{:S(2)}) copy-start(f32[12,128]{1,0:T(8,128)} %get-tuple-element.64) | copy-start | bytes 18436
  13.7 19.0 %all-to-all-start = ((f32[32,8,128]{2,1,0:T(8,128)}), f32[32,8,128]{2,1,0:T(8,128)S(1)}, u32[]{:S(2)}, u32[]{:S(2)}) async-start(f32[32,8,128]{2,1,0:T(8,128)} %get-tuple-element.73), calls=%async_computation | async-start | bytes 262144 | tf_op jit(solution)/shard_map/all_to_all | solution.py:445
  18.7 6.3 %collective-permute-start.6 = (f32[6,8,128]{2,1,0:T(8,128)S(1)}, f32[6,8,128]{2,1,0:T(8,128)S(1)}, u32[]{:S(2)}, u32[]{:S(2)}) collective-permute-start(f32[6,8,128]{2,1,0:T(8,128)S(1)} %copy-done.29), channel_id=1, source_target_pairs={{0,8},{8,0},{16,24},{24,16},{1,9},{9,1},{17,25},{25,17},{2,10},{10... | collective-permute-start | bytes 73736 | tf_op jit(solution)/shard_map/ppermute | solution.py:440
  20.6 4.5 %collective-permute-start.7 = (f32[6,8,128]{2,1,0:T(8,128)S(1)}, f32[6,8,128]{2,1,0:T(8,128)S(1)}, u32[]{:S(2)}, u32[]{:S(2)}) collective-permute-start(f32[6,8,128]{2,1,0:T(8,128)S(1)} %copy-done.28), channel_id=1, source_target_pairs={{0,1},{1,0},{2,3},{3,2},{4,5},{5,4},{6,7},{7,6},{8,16},{9,17},{10,... | collective-permute-start | bytes 73736 | tf_op jit(solution)/shard_map/ppermute | solution.py:441
  20.6 2.6 %collective-permute-start.4 = (f32[12,128]{1,0:T(8,128)S(1)}, f32[12,128]{1,0:T(8,128)S(1)}, u32[]{:S(2)}, u32[]{:S(2)}) collective-permute-start(f32[12,128]{1,0:T(8,128)S(1)} %copy-done.33), channel_id=1, source_target_pairs={{0,1},{1,0},{2,3},{3,2},{4,5},{5,4},{6,7},{7,6},{8,9},{9,8},{10,11... | collective-permute-start | bytes 18440 | tf_op jit(solution)/shard_map/ppermute | solution.py:438
  21.1 4.0 %collective-permute-start.5 = (f32[12,128]{1,0:T(8,128)S(1)}, f32[12,128]{1,0:T(8,128)S(1)}, u32[]{:S(2)}, u32[]{:S(2)}) collective-permute-start(f32[12,128]{1,0:T(8,128)S(1)} %copy-done.32), channel_id=1, source_target_pairs={{0,7},{1,2},{2,1},{3,4},{4,3},{5,6},{6,5},{7,0},{8,15},{9,10},{10,... | collective-permute-start | bytes 18440 | tf_op jit(solution)/shard_map/ppermute | solution.py:439
  23.1 2.0 %copy-start.8 = (f32[12,128]{1,0:T(8,128)}, f32[12,128]{1,0:T(8,128)S(1)}, u32[]{:S(2)}) copy-start(f32[12,128]{1,0:T(8,128)S(1)} %collective-permute-done.4.fa.fa1) | copy-start | bytes 18436
  25.1 0.6 copy-start.5
  27.4 8.0 %collective-permute-start.10 = (f32[6,8,128]{2,1,0:T(8,128)}, f32[6,8,128]{2,1,0:T(8,128)S(1)}, u32[]{:S(2)}, u32[]{:S(2)}) collective-permute-start(f32[6,8,128]{2,1,0:T(8,128)} %get-tuple-element.71), channel_id=1, source_target_pairs={{0,8},{8,0},{16,24},{24,16},{1,9},{9,1},{17,25},{25,17},{2,10},{10... | collective-permute-start | bytes 73736 | tf_op jit(solution)/shard_map/ppermute | solution.py:440
  30.0 5.5 %collective-permute-start.11 = (f32[6,8,128]{2,1,0:T(8,128)}, f32[6,8,128]{2,1,0:T(8,128)S(1)}, u32[]{:S(2)}, u32[]{:S(2)}) collective-permute-start(f32[6,8,128]{2,1,0:T(8,128)} %get-tuple-element.72), channel_id=1, source_target_pairs={{0,1},{1,0},{2,3},{3,2},{4,5},{5,4},{6,7},{7,6},{8,16},{9,17},{10,... | collective-permute-start | bytes 73736 | tf_op jit(solution)/shard_map/ppermute | solution.py:441
  30.0 5.5 %collective-permute-start.8 = (f32[12,128]{1,0:T(8,128)}, f32[12,128]{1,0:T(8,128)S(1)}, u32[]{:S(2)}, u32[]{:S(2)}) collective-permute-start(f32[12,128]{1,0:T(8,128)} %get-tuple-element.69), channel_id=1, source_target_pairs={{0,1},{1,0},{2,3},{3,2},{4,5},{5,4},{6,7},{7,6},{8,9},{9,8},{10,11... | collective-permute-start | bytes 18440 | tf_op jit(solution)/shard_map/ppermute | solution.py:438
  30.5 5.0 %collective-permute-start.9 = (f32[12,128]{1,0:T(8,128)}, f32[12,128]{1,0:T(8,128)S(1)}, u32[]{:S(2)}, u32[]{:S(2)}) collective-permute-start(f32[12,128]{1,0:T(8,128)} %get-tuple-element.70), channel_id=1, source_target_pairs={{0,7},{1,2},{2,1},{3,4},{4,3},{5,6},{6,5},{7,0},{8,15},{9,10},{10,... | collective-permute-start | bytes 18440 | tf_op jit(solution)/shard_map/ppermute | solution.py:439
  32.7 0.7 copy-start
  35.5 0.6 copy-start.11
  38.0 2.8 %copy-start.27 = (f32[6,8,128]{2,1,0:T(8,128)S(1)}, f32[6,8,128]{2,1,0:T(8,128)}, u32[]{:S(2)}) copy-start(f32[6,8,128]{2,1,0:T(8,128)} %get-tuple-element.82) | copy-start | bytes 73732
  38.0 4.5 %copy-start.26 = (f32[6,8,128]{2,1,0:T(8,128)S(1)}, f32[6,8,128]{2,1,0:T(8,128)}, u32[]{:S(2)}) copy-start(f32[6,8,128]{2,1,0:T(8,128)} %get-tuple-element.83) | copy-start | bytes 73732
  38.1 4.5 %copy-start.31 = (f32[12,128]{1,0:T(8,128)S(1)}, f32[12,128]{1,0:T(8,128)}, u32[]{:S(2)}) copy-start(f32[12,128]{1,0:T(8,128)} %get-tuple-element.80) | copy-start | bytes 18436
  38.1 5.0 %copy-start.30 = (f32[12,128]{1,0:T(8,128)S(1)}, f32[12,128]{1,0:T(8,128)}, u32[]{:S(2)}) copy-start(f32[12,128]{1,0:T(8,128)} %get-tuple-element.81) | copy-start | bytes 18436
  38.1 16.7 %all-to-all-start.1 = ((f32[32,2,128]{2,1,0:T(2,128)}), f32[32,2,128]{2,1,0:T(2,128)S(1)}, u32[]{:S(2)}, u32[]{:S(2)}) async-start(f32[32,2,128]{2,1,0:T(2,128)} %get-tuple-element.90), calls=%async_computation.1 | async-start | bytes 65536 | tf_op jit(solution)/shard_map/all_to_all | solution.py:445
  40.8 6.3 %collective-permute-start.14 = (f32[6,8,128]{2,1,0:T(8,128)S(1)}, f32[6,8,128]{2,1,0:T(8,128)S(1)}, u32[]{:S(2)}, u32[]{:S(2)}) collective-permute-start(f32[6,8,128]{2,1,0:T(8,128)S(1)} %copy-done.27), channel_id=1, source_target_pairs={{0,8},{8,0},{16,24},{24,16},{1,9},{9,1},{17,25},{25,17},{2,10},{10... | collective-permute-start | bytes 73736 | tf_op jit(solution)/shard_map/ppermute | solution.py:440
  42.5 4.5 %collective-permute-start.15 = (f32[6,8,128]{2,1,0:T(8,128)S(1)}, f32[6,8,128]{2,1,0:T(8,128)S(1)}, u32[]{:S(2)}, u32[]{:S(2)}) collective-permute-start(f32[6,8,128]{2,1,0:T(8,128)S(1)} %copy-done.26), channel_id=1, source_target_pairs={{0,1},{1,0},{2,3},{3,2},{4,5},{5,4},{6,7},{7,6},{8,16},{9,17},{10,... | collective-permute-start | bytes 73736 | tf_op jit(solution)/shard_map/ppermute | solution.py:441
  42.6 2.6 %collective-permute-start.12 = (f32[12,128]{1,0:T(8,128)S(1)}, f32[12,128]{1,0:T(8,128)S(1)}, u32[]{:S(2)}, u32[]{:S(2)}) collective-permute-start(f32[12,128]{1,0:T(8,128)S(1)} %copy-done.31), channel_id=1, source_target_pairs={{0,1},{1,0},{2,3},{3,2},{4,5},{5,4},{6,7},{7,6},{8,9},{9,8},{10,11... | collective-permute-start | bytes 18440 | tf_op jit(solution)/shard_map/ppermute | solution.py:438
  43.1 4.0 %collective-permute-start.13 = (f32[12,128]{1,0:T(8,128)S(1)}, f32[12,128]{1,0:T(8,128)S(1)}, u32[]{:S(2)}, u32[]{:S(2)}) collective-permute-start(f32[12,128]{1,0:T(8,128)S(1)} %copy-done.30), channel_id=1, source_target_pairs={{0,7},{1,2},{2,1},{3,4},{4,3},{5,6},{6,5},{7,0},{8,15},{9,10},{10,... | collective-permute-start | bytes 18440 | tf_op jit(solution)/shard_map/ppermute | solution.py:439
  45.2 1.9 %copy-start.22 = (f32[12,128]{1,0:T(8,128)}, f32[12,128]{1,0:T(8,128)S(1)}, u32[]{:S(2)}) copy-start(f32[12,128]{1,0:T(8,128)S(1)} %collective-permute-done.12.fa) | copy-start | bytes 18436
  47.1 0.6 copy-start.14
  47.1 0.6 copy-start.16
  49.4 7.7 %collective-permute-start.18 = (f32[6,8,128]{2,1,0:T(8,128)}, f32[6,8,128]{2,1,0:T(8,128)S(1)}, u32[]{:S(2)}, u32[]{:S(2)}) collective-permute-start(f32[6,8,128]{2,1,0:T(8,128)} %get-tuple-element.88), channel_id=1, source_target_pairs={{0,8},{8,0},{16,24},{24,16},{1,9},{9,1},{17,25},{25,17},{2,10},{10... | collective-permute-start | bytes 73736 | tf_op jit(solution)/shard_map/ppermute | solution.py:440
  52.0 5.2 %collective-permute-start.19 = (f32[6,8,128]{2,1,0:T(8,128)}, f32[6,8,128]{2,1,0:T(8,128)S(1)}, u32[]{:S(2)}, u32[]{:S(2)}) collective-permute-start(f32[6,8,128]{2,1,0:T(8,128)} %get-tuple-element.89), channel_id=1, source_target_pairs={{0,1},{1,0},{2,3},{3,2},{4,5},{5,4},{6,7},{7,6},{8,16},{9,17},{10,... | collective-permute-start | bytes 73736 | tf_op jit(solution)/shard_map/ppermute | solution.py:441
  52.1 5.1 %collective-permute-start.16 = (f32[12,128]{1,0:T(8,128)}, f32[12,128]{1,0:T(8,128)S(1)}, u32[]{:S(2)}, u32[]{:S(2)}) collective-permute-start(f32[12,128]{1,0:T(8,128)} %get-tuple-element.86), channel_id=1, source_target_pairs={{0,1},{1,0},{2,3},{3,2},{4,5},{5,4},{6,7},{7,6},{8,9},{9,8},{10,11... | collective-permute-start | bytes 18440 | tf_op jit(solution)/shard_map/ppermute | solution.py:438
  52.6 4.6 %collective-permute-start.17 = (f32[12,128]{1,0:T(8,128)}, f32[12,128]{1,0:T(8,128)S(1)}, u32[]{:S(2)}, u32[]{:S(2)}) collective-permute-start(f32[12,128]{1,0:T(8,128)} %get-tuple-element.87), channel_id=1, source_target_pairs={{0,7},{1,2},{2,1},{3,4},{4,3},{5,6},{6,5},{7,0},{8,15},{9,10},{10,... | collective-permute-start | bytes 18440 | tf_op jit(solution)/shard_map/ppermute | solution.py:439
  54.7 0.6 copy-start.1
  57.2 0.6 copy-start.12
  57.2 0.6 copy-start.13
  59.6 4.8 %collective-permute-start.22 = (f32[6,8,128]{2,1,0:T(8,128)}, f32[6,8,128]{2,1,0:T(8,128)S(1)}, u32[]{:S(2)}, u32[]{:S(2)}) collective-permute-start(f32[6,8,128]{2,1,0:T(8,128)} %get-tuple-element.99), channel_id=1, source_target_pairs={{0,8},{8,0},{16,24},{24,16},{1,9},{9,1},{17,25},{25,17},{2,10},{10... | collective-permute-start | bytes 73736 | tf_op jit(solution)/shard_map/ppermute | solution.py:440
  59.6 4.8 %collective-permute-start.23 = (f32[6,8,128]{2,1,0:T(8,128)}, f32[6,8,128]{2,1,0:T(8,128)S(1)}, u32[]{:S(2)}, u32[]{:S(2)}) collective-permute-start(f32[6,8,128]{2,1,0:T(8,128)} %get-tuple-element.100), channel_id=1, source_target_pairs={{0,1},{1,0},{2,3},{3,2},{4,5},{5,4},{6,7},{7,6},{8,16},{9,17},{10,... | collective-permute-start | bytes 73736 | tf_op jit(solution)/shard_map/ppermute | solution.py:441
  59.7 2.2 %collective-permute-start.20 = (f32[12,128]{1,0:T(8,128)}, f32[12,128]{1,0:T(8,128)S(1)}, u32[]{:S(2)}, u32[]{:S(2)}) collective-permute-start(f32[12,128]{1,0:T(8,128)} %get-tuple-element.97), channel_id=1, source_target_pairs={{0,1},{1,0},{2,3},{3,2},{4,5},{5,4},{6,7},{7,6},{8,9},{9,8},{10,11... | collective-permute-start | bytes 18440 | tf_op jit(solution)/shard_map/ppermute | solution.py:438
  60.2 4.2 %collective-permute-start.21 = (f32[12,128]{1,0:T(8,128)}, f32[12,128]{1,0:T(8,128)S(1)}, u32[]{:S(2)}, u32[]{:S(2)}) collective-permute-start(f32[12,128]{1,0:T(8,128)} %get-tuple-element.98), channel_id=1, source_target_pairs={{0,7},{1,2},{2,1},{3,4},{4,3},{5,6},{6,5},{7,0},{8,15},{9,10},{10,... | collective-permute-start | bytes 18440 | tf_op jit(solution)/shard_map/ppermute | solution.py:439
  61.9 2.5 %copy-start.23 = (f32[12,128]{1,0:T(8,128)}, f32[12,128]{1,0:T(8,128)S(1)}, u32[]{:S(2)}) copy-start(f32[12,128]{1,0:T(8,128)S(1)} %collective-permute-done.20.fa) | copy-start | bytes 18436
  64.4 0.6 copy-start.15
  (12 other events, 7.2 us)
